TPU v7x, 1024 devices: a whole 4x8x16 slice. The times are simulated.
1024 devices in a mesh: group: 64 (over x, z), head: 8 (over y_hi, core), hid: 2 (over y_lo).
Axes of the slice: x: 4, y: 8 (y_hi: 4, y_lo: 2; y = y_hi * 2 + y_lo), z: 16, core: 2. Of those that a mesh axis runs over, the one named last changes fastest.
Arguments:
- tokens: bfloat16 [16384, 5120], P(('group', 'head', 'hid')), may hold values from -6 to 6
- w_query: bfloat16 [5120, 4096], P('group', ('head', 'hid')), may hold values from -0.078125 to 0.078125
- keyval_weight: bfloat16 [5120, 8, 256], P(('group', 'hid'), 'head'), may hold values from -0.078125 to 0.078125
- q_gain: float32 [128], replicated, may hold values from 0.1 to 1.9
- k_gain: float32 [128], replicated, may hold values from 0.1 to 1.9
- segments: int32 [64, 256], P('group'), may hold values from 0 to 3, never falling along the last dimension, each value on 1 to 128 neighbouring positions
Outputs:
- attention: bfloat16 [16384, 4096], P('group', ('head', 'hid'))
- kv_cache: bfloat16 [16384, 8, 256], P('group', 'head')
Inputs may be any that keep to these rules, and one draw needn't show every extreme that they name: `segments`: within each replica's 256 tokens segment numbers never fall; each of the 4 sequences holds 1 to 128 tokens and one holds exactly 128.
All inputs are finite; a program needn't handle non-finite values.
Results may differ from a plain program's by a relative error of at most 0.0068.
Values may be sent and summed in bfloat16 or wider, within the bound.
No kernel may reach another device: no remote copies, remote signals or barrier semaphores. Data moves between devices by JAX's collectives and lax.ppermute only.
A program may use at most 32 MiB of HBM per device.

v0:
```python
import jax
import jax.numpy as jnp
from jax import lax
from jax.sharding import PartitionSpec as P

QUERY_HEADS = 32
KEYVAL_HEADS = 8


theta_base = 1000000.0
epsilon = 1e-06


def head_norm(values, gain):
    return values * lax.rsqrt(jnp.mean(values * values, axis=-1, keepdims=True) + epsilon) * gain


def rotate(values, places):
    width = values.shape[-1]
    half = width // 2
    index = jnp.arange(half, dtype=jnp.float32)
    freqs = jnp.power(theta_base, -2.0 * index / width)
    angles = places.astype(jnp.float32)[:, None] * freqs[None, :]
    cosine = jnp.cos(angles)[:, None, :]
    sine = jnp.sin(angles)[:, None, :]
    first_half = values[..., :half]
    second_half = values[..., half:]
    return jnp.concatenate(
        [first_half * cosine - second_half * sine, second_half * cosine + first_half * sine],
        axis=-1,
    )


def token_places(seg_ids):
    count_total = seg_ids.shape[0]
    before = jnp.sum((seg_ids[None, :] < seg_ids[:, None]).astype(jnp.int32), axis=1)
    return jnp.arange(count_total, dtype=jnp.int32) - before


def attend(query_rot, key_heads, value_heads, seg_ids):
    count_total = query_rot.shape[0]
    width = query_rot.shape[-1]
    scores = jnp.einsum(
        "qhd,khd->hqk", query_rot, key_heads, preferred_element_type=jnp.float32
    ) / jnp.sqrt(jnp.float32(width))
    index = jnp.arange(count_total, dtype=jnp.int32)
    allowed = (index[None, :] <= index[:, None]) & (seg_ids[None, :] == seg_ids[:, None])
    masked = jnp.where(allowed[None], scores, jnp.float32(-1e30))
    peak = jnp.max(masked, axis=-1, keepdims=True)
    expd = jnp.where(allowed[None], jnp.exp(masked - peak), jnp.float32(0.0))
    probs = (expd / jnp.sum(expd, axis=-1, keepdims=True)).astype(jnp.bfloat16)
    output = jnp.einsum("hqk,khd->qhd", probs, value_heads, preferred_element_type=jnp.float32)
    return output.astype(jnp.bfloat16).reshape(count_total, -1)


def body(tokens, w_query, keyval_weight, q_gain, k_gain, segments):
    kv_local = keyval_weight.shape[1]
    pair_width = keyval_weight.shape[2]
    head_size = pair_width // 2
    whole = lax.all_gather(tokens, ("head", "hid"), axis=0, tiled=True)
    count_total = whole.shape[0]

    def add_rows(piece):
        return jnp.dot(whole, piece.reshape(piece.shape[0], -1), preferred_element_type=jnp.float32)

    query = add_rows(lax.all_gather(w_query, "group", axis=0, tiled=True))
    key_value = add_rows(lax.all_gather(keyval_weight, ("group", "hid"), axis=0, tiled=True))
    seg_ids = segments.reshape(-1)
    places = token_places(seg_ids)
    key_value = key_value.reshape(count_total, kv_local, pair_width)
    key_rot = rotate(head_norm(key_value[..., :head_size], k_gain), places).astype(jnp.bfloat16)
    value_b = key_value[..., head_size:].astype(jnp.bfloat16)
    cache_store = jnp.concatenate([key_rot, value_b], axis=-1)
    q_local = query.shape[1] // head_size
    query_rot = rotate(
        head_norm(query.reshape(count_total, q_local, head_size), q_gain), places
    ).astype(jnp.bfloat16)
    group_ratio = QUERY_HEADS // KEYVAL_HEADS
    head_first = (lax.axis_index("head") * lax.axis_size("hid") + lax.axis_index("hid")) * q_local
    which_head = (
        head_first + jnp.arange(q_local, dtype=jnp.int32)
    ) // group_ratio - lax.axis_index("head") * kv_local
    key_heads = jnp.take(key_rot, which_head, axis=1)
    value_heads = jnp.take(value_b, which_head, axis=1)
    attention = attend(query_rot, key_heads, value_heads, seg_ids)
    return (attention, cache_store)


def solution(mesh):
    return jax.shard_map(
        body,
        mesh=mesh,
        in_specs=(
            P(("group", "head", "hid"), None),
            P("group", ("head", "hid")),
            P(("group", "hid"), "head", None),
            P(),
            P(),
            P("group", None),
        ),
        out_specs=(P("group", ("head", "hid")), P("group", "head", None)),
        check_vma=False,
    )
```

profile of v0, /device:TPU:16, one launch (start us, length us, event | category | flops | bytes accessed | tf_op | source)
XLA Modules:
  0.0 848.4 jit_solution(14113653029503940454)
XLA Ops:
  7.2 0.0 all-gather.4.cloned.1.call-start
  7.2 0.7 all-gather.4.cloned.1.call-update
  7.9 0.0 all-gather.8.cloned.1.call-start
  7.9 0.7 all-gather.8.cloned.1.call-update
  8.6 0.0 all-gather.6.cloned.1.call-start
  8.7 0.7 all-gather.6.cloned.1.call-update
  9.4 0.9 convert_reduce_fusion
  10.3 0.9 fusion.10
  11.2 0.5 multiply_cosine_fusion
  11.7 0.0 copy-start.1
  11.7 76.3 %all-gather.4.cloned.1.call-done = bf16[256,5120]{1,0:T(8,128)(2,1)} async-done(((bf16[16,5120]{1,0:T(8,128)(2,1)}), bf16[256,5120]{1,0:T(8,128)(2,1)}) %all-gather.4.cloned.1.call-update) | async-done | bytes 2621456 | tf_op jit(solution)/shard_map/all_gather | solution.py:60
  88.0 0.0 copy-start
  88.0 153.8 %all-gather.8.cloned.1.call-done = bf16[5120,256]{1,0:T(8,128)(2,1)} async-done(((bf16[80,256]{1,0:T(8,128)(2,1)}), bf16[5120,256]{1,0:T(8,128)(2,1)}) %all-gather.8.cloned.1.call-update) | async-done | bytes 2621456 | tf_op jit(solution)/shard_map/all_gather | solution.py:66
  241.8 3.7 multiply_reduce_fusion
  245.5 0.1 copy.8
  245.7 0.0 copy-done.1
  245.7 0.1 multiply_multiply_fusion
  245.8 0.2 subtract_convert_fusion
  246.0 0.0 copy-start.2
  246.0 589.7 %all-gather.6.cloned.1.call-done = bf16[5120,1,256]{2,0,1:T(8,128)(2,1)} async-done(((bf16[40,1,256]{2,0,1:T(8,128)(2,1)}), bf16[5120,1,256]{2,0,1:T(8,128)(2,1)}) %all-gather.6.cloned.1.call-update) | async-done | bytes 2621456 | tf_op jit(solution)/shard_map/all_gather | solution.py:67
  835.7 0.0 copy-done
  835.7 2.9 fusion.7
  838.6 0.0 copy-done.2
  838.6 0.1 multiply_multiply_fusion.1
  838.7 0.3 fusion.23
  839.1 0.1 copy.9
  839.2 0.5 fusion.45
  839.6 0.3 fusion.6
  840.0 0.8 copy.12
  840.7 0.3 convolution_convert_fusion
  841.1 0.8 copy.11
  (10 shorter events, 0.1 us)
Async XLA Ops:
  7.2 80.9 %all-gather.4.cloned.1.call-start = ((), (), s32[]{:S(2)}) async-start(), calls=%async_computation | async-start | bytes 2785280 | tf_op jit(solution)/shard_map/all_gather | solution.py:60
  7.9 233.9 %all-gather.8.cloned.1.call-start = ((), (), s32[]{:S(2)}) async-start(), calls=%async_computation.2 | async-start | bytes 2662400 | tf_op jit(solution)/shard_map/all_gather | solution.py:66
  8.6 827.0 %all-gather.6.cloned.1.call-start = ((), (), s32[]{:S(2)}) async-start(), calls=%async_computation.1 | async-start | bytes 2641920 | tf_op jit(solution)/shard_map/all_gather | solution.py:67
  11.7 234.0 %copy-start.1 = (f32[128]{0:T(128)S(1)}, f32[128]{0:T(128)}, u32[]{:S(2)}) copy-start(f32[128]{0:T(128)} %param.11) | copy-start | bytes 1540
  88.0 747.6 %copy-start = (bf16[256,5120]{1,0:T(8,128)(2,1)S(1)}, bf16[256,5120]{1,0:T(8,128)(2,1)}, u32[]{:S(2)}) copy-start(bf16[256,5120]{1,0:T(8,128)(2,1)} %all-gather.4.cloned.1.call-done) | copy-start | bytes 7864324
  246.0 592.6 %copy-start.2 = (f32[128]{0:T(128)S(1)}, f32[128]{0:T(128)}, u32[]{:S(2)}) copy-start(f32[128]{0:T(128)} %param.12) | copy-start | bytes 1540
Sparse Core Ops, SparseCore 0:
  10.7 77.3 all-gather.3
  92.2 149.6 all-gather.7
  244.5 591.0 all-gather.5
where the time goes:
time: 849 us; the launch traced here: 848 us
  waiting for transfers between devices  822 us (97%)
  between operations  13.9 us (2%)
    all_gather x1, waiting for transfers between devices, body(): lax.all_gather(keyval_weight, ('group', 'hid'), axis=0, tiled=True)  590 us
    all_gather x1, waiting for transfers between devices, body(): query = add_rows(lax.all_gather(w_query, 'group', axis=0, tiled=True))  154 us
    all_gather x1, waiting for transfers between devices, body(): whole = lax.all_gather(tokens, ('head', 'hid'), axis=0, tiled=True)  76.3 us
  transfers between devices with their start and end apart: 3, of which 3 were waited for; matrix products, arithmetic and copies ran while one was open for 1% of the time, Pallas kernels for 0%

commit v1 on v0

v1 whole, which is shorter than its diff:
```python
import jax
import jax.numpy as jnp
from jax import lax
from jax.sharding import Mesh, PartitionSpec as P

QUERY_HEADS = 32
KEYVAL_HEADS = 8

theta_base = 1000000.0
epsilon = 1e-06

N_X, N_Z, N_YH, N_CORE, N_YL = 4, 16, 4, 2, 2


def head_norm(values, gain):
    return values * lax.rsqrt(jnp.mean(values * values, axis=-1, keepdims=True) + epsilon) * gain


def rotate(values, cosine, sine):
    half = values.shape[-1] // 2
    first_half = values[..., :half]
    second_half = values[..., half:]
    return jnp.concatenate(
        [first_half * cosine - second_half * sine, second_half * cosine + first_half * sine],
        axis=-1,
    )


def token_places(seg_ids):
    count_total = seg_ids.shape[0]
    before = jnp.sum((seg_ids[None, :] < seg_ids[:, None]).astype(jnp.int32), axis=1)
    return jnp.arange(count_total, dtype=jnp.int32) - before


def attend(query_rot, key_rot, value_b, seg_ids):
    count_total = query_rot.shape[0]
    width = query_rot.shape[-1]
    scores = jnp.einsum(
        "qhd,kd->hqk", query_rot, key_rot, preferred_element_type=jnp.float32
    ) / jnp.sqrt(jnp.float32(width))
    index = jnp.arange(count_total, dtype=jnp.int32)
    allowed = (index[None, :] <= index[:, None]) & (seg_ids[None, :] == seg_ids[:, None])
    masked = jnp.where(allowed[None], scores, jnp.float32(-1e30))
    peak = jnp.max(masked, axis=-1, keepdims=True)
    expd = jnp.where(allowed[None], jnp.exp(masked - peak), jnp.float32(0.0))
    probs = (expd / jnp.sum(expd, axis=-1, keepdims=True)).astype(jnp.bfloat16)
    output = jnp.einsum("hqk,kd->qhd", probs, value_b, preferred_element_type=jnp.float32)
    return output.astype(jnp.bfloat16).reshape(count_total, -1)


def body(tokens, w_query, keyval_weight, q_gain, k_gain, segments):
    q_rows, q_cols = w_query.shape
    kv_rows, _, pair_width = keyval_weight.shape
    head_size = pair_width // 2
    near = lax.axis_index("yl")

    whole = lax.all_gather(tokens, ("yh", "core", "yl"), axis=0, tiled=True)

    block = jnp.concatenate([w_query, keyval_weight.reshape(kv_rows, pair_width)], axis=0)
    column = lax.all_gather(block, "z", axis=0)
    plane = lax.all_to_all(
        jnp.broadcast_to(column[None], (N_X, *column.shape)), "x", split_axis=0, concat_axis=0
    ).reshape(N_X * N_Z, q_rows + kv_rows, q_cols)
    wq = plane[:, :q_rows].reshape(-1, q_cols)
    wkv = lax.dynamic_update_slice(
        jnp.zeros((N_X * N_Z, N_YL * kv_rows, pair_width), jnp.bfloat16),
        plane[:, q_rows:],
        (0, near * kv_rows, 0),
    ).reshape(-1, pair_width)

    def product(weight):
        return jnp.dot(whole, weight, preferred_element_type=jnp.float32)

    partial = product(wkv)
    key_value = partial + lax.ppermute(partial, "yl", [(0, 1), (1, 0)])
    query = product(wq)
    count_total = query.shape[0]

    seg_ids = segments.reshape(-1)
    places = token_places(seg_ids)
    half = head_size // 2
    freqs = jnp.power(theta_base, -2.0 * jnp.arange(half, dtype=jnp.float32) / head_size)
    angles = places.astype(jnp.float32)[:, None] * freqs[None, :]
    cosine, sine = jnp.cos(angles), jnp.sin(angles)
    key_rot = rotate(head_norm(key_value[:, :head_size], k_gain), cosine, sine).astype(jnp.bfloat16)
    value_b = key_value[:, head_size:].astype(jnp.bfloat16)
    cache_store = jnp.concatenate([key_rot, value_b], axis=-1)[:, None, :]
    query_rot = rotate(
        head_norm(query.reshape(count_total, -1, head_size), q_gain), cosine[:, None, :], sine[:, None, :]
    ).astype(jnp.bfloat16)
    return (attend(query_rot, key_rot, value_b, seg_ids), cache_store)


def solution(mesh):
    fine = Mesh(
        mesh.devices.reshape(N_X, N_Z, N_YH, N_CORE, N_YL), ("x", "z", "yh", "core", "yl")
    )
    group, head = ("x", "z"), ("yh", "core")
    return jax.shard_map(
        body,
        mesh=fine,
        in_specs=(
            P((*group, *head, "yl"), None),
            P(group, (*head, "yl")),
            P((*group, "yl"), head, None),
            P(),
            P(),
            P(group, None),
        ),
        out_specs=(P(group, (*head, "yl")), P(group, head, None)),
        check_vma=False,
    )
```

time: 849 us -> 133 us (0.16)
  the two profiles are of different devices: /device:TPU:16 before, /device:TPU:32 now
where the time goes in v1:
time: 133 us; the launch traced here: 132 us
  blocking collectives  48 us (36%)
  waiting for transfers between devices  45.8 us (34%)
  between operations  14.2 us (11%)
  local copies, waits for them, and re-layouts  10.1 us (8%)
  starting transfers between devices  6.89 us (5%)
  matrix products  5.59 us (4%)
  other arithmetic  1.83 us (1%)
    all_gather x1, blocking collectives, body(): column = lax.all_gather(block, 'z', axis=0)  48 us
    all_to_all x1, waiting for transfers between devices, body(): lax.all_to_all(jnp.broadcast_to(column[None], (N_X, *column.shape)), 'x',...  40 us
    ppermute x1, waiting for transfers between devices, body(): key_value = partial + lax.ppermute(partial, 'yl', [(0, 1), (1, 0)])  5.06 us
    all_to_all x1, starting transfers between devices, body(): lax.all_to_all(jnp.broadcast_to(column[None], (N_X, *column.shape)), 'x',...  4.94 us
    dot_general x2, matrix products, product(): return jnp.dot(whole, weight, preferred_element_type=jnp.float32)  4.51 us
  transfers between devices with their start and end apart: 3, of which 2 were waited for; matrix products, arithmetic and copies ran while one was open for 8% of the time, Pallas kernels for 0%

profile of v1, /device:TPU:32, one launch (start us, length us, event | category | flops | bytes accessed | tf_op | source)
XLA Modules:
  0.0 132.4 jit_solution(14670033566505623719)
XLA Ops:
  7.2 0.0 all-gather.3.cloned.1.call-start
  7.2 0.7 all-gather.3.cloned.1.call-update
  7.9 0.8 pad_maximum_fusion
  8.7 48.0 %all-gather = bf16[1920,256]{1,0:T(8,128)(2,1)S(1)} all-gather(bf16[120,256]{1,0:T(8,128)(2,1)S(1)} %pad_maximum_fusion), channel_id=2, replica_groups=mesh['x'=4,'z'=16,'yh'=4,'core'=2,'yl'=2] {'z'}, dimensions={0}, use_global_device_ids=true | all-gather | bytes 1044480 | tf_op jit(solution)/shard_map/all_gather | solution.py:60
  56.7 2.2 %broadcast_in_dim.25 = bf16[4,16,120,256]{3,2,1,0:T(8,128)(2,1)} broadcast(bf16[16,120,256]{2,1,0:T(8,128)(2,1)S(1)} %bitcast.51), dimensions={1,2,3} | broadcast | bytes 4915200 | tf_op jit(solution)/shard_map/broadcast_in_dim | solution.py:62
  58.8 0.0 copy-start
  58.8 4.9 %all-to-all-start = ((bf16[4,16,120,256]{3,2,1,0:T(8,128)(2,1)}), bf16[4,16,120,256]{3,2,1,0:T(8,128)(2,1)}, u32[]{:S(2)}, u32[]{:S(2)}) async-start(bf16[4,16,120,256]{3,2,1,0:T(8,128)(2,1)} %broadcast_in_dim.25), calls=%async_computation | async-start | bytes 7864320 | tf_op jit(solution)/shard_map/all_to_all | solution.py:61
  63.8 0.0 copy-done
  63.8 0.1 convert_reduce_fusion
  63.9 0.1 fusion.6
  64.1 40.0 %all-to-all-done = bf16[4,16,120,256]{3,2,1,0:T(8,128)(2,1)} async-done(((bf16[4,16,120,256]{3,2,1,0:T(8,128)(2,1)}), bf16[4,16,120,256]{3,2,1,0:T(8,128)(2,1)}, u32[]{:S(2)}, u32[]{:S(2)}) %all-to-all-start) | async-done | bytes 3932192 | tf_op jit(solution)/shard_map/all_to_all | solution.py:61
  104.1 1.9 %slice.38 = bf16[64,80,256]{2,1,0:T(8,128)(2,1)S(1)} slice(bf16[64,120,256]{2,1,0:T(8,128)(2,1)} %bitcast.2), slice={[0:64], [0:80], [0:256]} | slice | bytes 5242880 | tf_op jit(solution)/shard_map/slice | solution.py:64
  106.0 1.7 %broadcast_in_dim.20 = bf16[64,80,256]{2,1,0:T(8,128)(2,1)} broadcast(bf16[]{:T(256)} %constant.13.clone.1), dimensions={} | broadcast | bytes 2621442 | tf_op jit(solution)/shard_map/broadcast_in_dim | solution.py:66
  107.7 2.5 %slice_dynamic-update-slice_fusion = bf16[64,80,256]{2,1,0:T(8,128)(2,1)} fusion(bf16[64,80,256]{2,1,0:T(8,128)(2,1)} %broadcast_in_dim.20, s32[]{:T(128)S(6)} %select_n.10, bf16[64,120,256]{2,1,0:T(8,128)(2,1)} %bitcast.2), kind=kLoop, calls=%fused_computation.1 | loop fusion | bytes 2621444 | tf_op jit(solution)/shard_map/dynamic_update_slice | solution.py:65
  110.2 0.0 all-gather.3.cloned.1.call-done
  110.2 0.0 copy-start.3
  110.2 3.6 %convolution_bitcast_fusion = f32[256,256]{0,1:T(8,128)S(1)} fusion(bf16[5120,256]{1,0:T(8,128)(2,1)} %bitcast.3, bf16[256,5120]{1,0:T(8,128)(2,1)} %all-gather.3.cloned.1.call-done), kind=kOutput, calls=%fused_computation.8 | convolution fusion | flops 671088640 | bytes 5505024 | tf_op jit(solution)/shard_map/dot_general | solution.py:72
  113.7 1.9 %collective-permute-start = (f32[256,256]{0,1:T(8,128)S(1)}, f32[256,256]{0,1:T(8,128)S(1)}, u32[]{:S(2)}, u32[]{:S(2)}) collective-permute-start(f32[256,256]{0,1:T(8,128)S(1)} %convolution_bitcast_fusion), channel_id=1, source_target_pairs={{0,1},{1,0},{2,3},{3,2},{4,5},{5,4},{6,7},{7,6},{8,9},{9,8},{10,11... | collective-permute-start | bytes 786440 | tf_op jit(solution)/shard_map/ppermute | solution.py:75
  115.7 0.0 copy-done.3
  115.7 0.0 copy-start.1
  115.7 0.0 copy-start.2
  115.7 0.9 multiply_reduce_fusion
  116.7 0.1 copy.8
  116.8 0.0 copy-done.1
  116.8 0.1 multiply_multiply_fusion
  117.0 5.1 %collective-permute-done = f32[256,256]{0,1:T(8,128)S(1)} collective-permute-done((f32[256,256]{0,1:T(8,128)S(1)}, f32[256,256]{0,1:T(8,128)S(1)}, u32[]{:S(2)}, u32[]{:S(2)}) %collective-permute-start) | collective-permute-done | bytes 262176 | tf_op jit(solution)/shard_map/ppermute | solution.py:75
  122.1 0.0 copy-done.2
  122.1 0.1 multiply_multiply_fusion.1
  122.2 0.3 subtract_convert_fusion.1
  122.6 0.8 copy.14
  123.3 0.1 copy.10
  123.4 0.1 copy.9
  123.5 0.2 subtract_convert_fusion
  123.7 0.5 fusion.36
  124.2 0.6 convolution_convert_fusion
  124.8 0.8 copy.13
  (8 shorter events, 0.1 us)
Async XLA Ops:
  7.2 103.0 %all-gather.3.cloned.1.call-start = ((), (), s32[]{:S(2)}) async-start(), calls=%async_computation.1 | async-start | bytes 2785280 | tf_op jit(solution)/shard_map/all_gather | solution.py:57
  58.8 5.0 %copy-start = (s32[1,256]{1,0:T(1,128)S(1)}, s32[1,256]{1,0:T(1,128)}, u32[]{:S(2)}) copy-start(s32[1,256]{1,0:T(1,128)} %param.11) | copy-start | bytes 3076
  58.8 45.2 %all-to-all-start = ((bf16[4,16,120,256]{3,2,1,0:T(8,128)(2,1)}), bf16[4,16,120,256]{3,2,1,0:T(8,128)(2,1)}, u32[]{:S(2)}, u32[]{:S(2)}) async-start(bf16[4,16,120,256]{3,2,1,0:T(8,128)(2,1)} %broadcast_in_dim.25), calls=%async_computation | async-start | bytes 7864320 | tf_op jit(solution)/shard_map/all_to_all | solution.py:61
  110.2 5.5 %copy-start.3 = (bf16[256,5120]{1,0:T(8,128)(2,1)S(1)}, bf16[256,5120]{1,0:T(8,128)(2,1)}, u32[]{:S(2)}) copy-start(bf16[256,5120]{1,0:T(8,128)(2,1)} %all-gather.3.cloned.1.call-done) | copy-start | bytes 7864324
  113.7 8.3 %collective-permute-start = (f32[256,256]{0,1:T(8,128)S(1)}, f32[256,256]{0,1:T(8,128)S(1)}, u32[]{:S(2)}, u32[]{:S(2)}) collective-permute-start(f32[256,256]{0,1:T(8,128)S(1)} %convolution_bitcast_fusion), channel_id=1, source_target_pairs={{0,1},{1,0},{2,3},{3,2},{4,5},{5,4},{6,7},{7,6},{8,9},{9,8},{10,11... | collective-permute-start | bytes 786440 | tf_op jit(solution)/shard_map/ppermute | solution.py:75
  115.7 1.1 copy-start.1
  115.7 6.4 %copy-start.2 = (f32[128]{0:T(128)S(1)}, f32[128]{0:T(128)}, u32[]{:S(2)}) copy-start(f32[128]{0:T(128)} %param.10) | copy-start | bytes 1540
Sparse Core Ops, SparseCore 0:
  10.7 76.2 all-gather.2
